TPU v7x, 128 devices: a whole 4x4x4 slice. The times are simulated.
128 devices in a mesh: layer: 4 (over z), panel: 32 (over x, y, core).
Axes of the slice: x: 4, y: 4, z: 4, core: 2. Of those that a mesh axis runs over, the one named last changes fastest.
Arguments:
- reflections: float32 [32, 1024, 1024], P(None, 'panel'), may hold values from -0.95 to 0.95
- wave_decay: float32 [32, 1024], replicated, may hold values from 0.3 to 3
- thickness: float32 [4], P('layer'), may hold values from 0.4 to 1
- material: int32 [4], P('layer'), may hold values from 0 to 31
Outputs:
- stack_blocks: float32 [4, 1024, 1024], P('layer', 'panel')
All inputs are finite; a program needn't handle non-finite values.
Results may differ from a plain program's by a relative error of at most 0.00014.
Values sent between devices are 32-bit elements; how exact they have to be, the bound alone decides.
No kernel may reach another device: no remote copies, remote signals or barrier semaphores. Data moves between devices by JAX's collectives and lax.ppermute only.
A program may use at most 128 MiB of HBM per device.

v0:
```python
import jax
import jax.numpy as jnp
from jax import lax
from jax.sharding import PartitionSpec as P

TERMS = 6


def swapped(block, axis, bit):
    count = lax.axis_size(axis)
    route = []
    for low in range(count):
        high = low | 1 << bit
        if high != low and high < count:
            route += [(low, high), (high, low)]
    return lax.ppermute(block, axis, route)


def product(left_side, right_side):
    return jnp.dot(
        left_side, right_side, precision=lax.Precision.HIGHEST, preferred_element_type=jnp.float32
    )


def series_sum(start_rows, factor_one, factor_two):
    term_now = start_rows
    summed = start_rows
    for _ in range(TERMS - 1):
        term_now = product(product(term_now, factor_one), factor_two)
        summed = summed + term_now
    return summed


def local(reflections, wave_decay, thickness, material):
    panel_rows = reflections.shape[1]
    order_full = reflections.shape[2]
    row_start = lax.axis_index("panel") * panel_rows
    chosen = material[0]
    refl_rows = lax.dynamic_index_in_dim(reflections, chosen, 0, keepdims=False)
    decays = jnp.exp(
        -lax.dynamic_index_in_dim(wave_decay, chosen, 0, keepdims=False) * thickness[0]
    )
    refl_full = lax.all_gather(refl_rows, "panel", axis=0, tiled=True)
    scaled_refl = decays[:, None] * refl_full
    row_ids = row_start + jnp.arange(panel_rows, dtype=jnp.int32)
    identity_rows = jnp.where(
        row_ids[:, None] == jnp.arange(order_full, dtype=jnp.int32)[None, :], 1.0, 0.0
    ).astype(jnp.float32)
    summed = series_sum(identity_rows, scaled_refl, scaled_refl)
    numer = decays[:, None] * refl_full * decays[None, :] - refl_full
    reflect_block = product(summed, numer)
    scaled_sum = summed * decays[None, :]
    trans_block = scaled_sum - product(product(scaled_sum, refl_full), refl_full)
    blocks = (reflect_block, trans_block, trans_block, reflect_block)
    depth_count = lax.axis_size("layer").bit_length() - 1
    for depth_level in range(depth_count):
        partner_blocks = swapped((blocks[0], blocks[1], blocks[2], blocks[3]), "layer", depth_level)
        is_right = lax.axis_index("layer") // 2**depth_level % 2 == 1
        front_part = tuple((jnp.where(is_right, partner_blocks[i], blocks[i]) for i in range(4)))
        back_part = tuple((jnp.where(is_right, blocks[i], partner_blocks[i]) for i in range(4)))
        back_refl_full, front_refl_full, front_trans_full, back_trans_full = (
            lax.all_gather(back_part[0], "panel", axis=0, tiled=True),
            lax.all_gather(front_part[3], "panel", axis=0, tiled=True),
            lax.all_gather(front_part[2], "panel", axis=0, tiled=True),
            lax.all_gather(back_part[1], "panel", axis=0, tiled=True),
        )
        upper_chain = series_sum(front_part[1], back_refl_full, front_refl_full)
        lower_chain = series_sum(back_part[2], front_refl_full, back_refl_full)
        block_one = front_part[0] + product(product(upper_chain, back_refl_full), front_trans_full)
        block_two = product(upper_chain, back_trans_full)
        block_three = product(lower_chain, front_trans_full)
        block_four = back_part[3] + product(product(lower_chain, front_refl_full), back_trans_full)
        blocks = (block_one, block_two, block_three, block_four)
    stacked = jnp.stack(blocks)
    block_count = stacked.shape[0] // lax.axis_size("layer")
    return lax.dynamic_slice_in_dim(stacked, lax.axis_index("layer") * block_count, block_count, 0)


def solution(mesh):
    placed = (P(None, "panel", None), P(), P("layer"), P("layer"))
    return jax.shard_map(
        local, mesh=mesh, in_specs=placed, out_specs=P("layer", "panel", None), check_vma=False
    )
```

profile of v0, /device:TPU:1, one launch (start us, length us, event | category | flops | bytes accessed | tf_op | source)
XLA Modules:
  0.0 528.1 jit_solution(8382436333740291440)
XLA Ops:
  10.3 48.9 %all-gather.27.cloned.1.call-done = f32[1,1024,1024]{2,1,0:T(8,128)} async-done(((f32[1,32,1024]{2,1,0:T(8,128)}), f32[1,1024,1024]{2,1,0:T(8,128)}) %all-gather.27.cloned.1.call-update) | async-done | bytes 4194320 | tf_op jit(solution)/shard_map/all_gather | solution.py:43
  59.2 5.0 fusion.10
  88.6 15.6 %fusion.4 = f32[32,1024]{1,0:T(8,128)S(1)} fusion(f32[32,1024]{1,0:T(8,128)S(1)} %convolution_add_fusion.2, f32[1,1024,1024]{2,1,0:T(8,128)S(1)} %copy-done, f32[1024]{0:T(1024)S(1)} %bitcast.161), kind=kOutput, calls=%fused_computation.6 | convolution fusion | flops 405798912 | bytes 4460544 | tf_op jit(solution)/shard_map/dot_general | solution.py:20
  110.7 4.8 fusion.2
  123.3 32.9 %all-gather.11.cloned.1.call-done = f32[1024,1024]{1,0:T(8,128)} async-done(((f32[32,1024]{1,0:T(8,128)}), f32[1024,1024]{1,0:T(8,128)}) %all-gather.11.cloned.1.call-update) | async-done | bytes 4194320 | tf_op jit(solution)/shard_map/all_gather | solution.py:62
  156.2 4.7 fusion.35
  161.0 42.9 %all-gather.13.cloned.1.call-done = f32[1024,1024]{1,0:T(8,128)} async-done(((f32[32,1024]{1,0:T(8,128)}), f32[1024,1024]{1,0:T(8,128)}) %all-gather.13.cloned.1.call-update) | async-done | bytes 4194320 | tf_op jit(solution)/shard_map/all_gather | solution.py:63
  203.9 4.8 fusion.36
  231.6 19.9 %all-gather.15.cloned.1.call-done = f32[1024,1024]{1,0:T(8,128)} async-done(((f32[32,1024]{1,0:T(8,128)}), f32[1024,1024]{1,0:T(8,128)}) %all-gather.15.cloned.1.call-update) | async-done | bytes 4194320 | tf_op jit(solution)/shard_map/all_gather | solution.py:64
  251.5 4.8 convolution_add_fusion.1
  263.5 4.8 fusion.46
  293.7 5.3 all-gather.17.cloned.1.call-done
  299.0 4.8 convolution_add_fusion
  311.0 4.7 fusion.45
  321.1 25.4 %all-gather.19.cloned.1.call-done = f32[1024,1024]{1,0:T(8,128)} async-done(((f32[32,1024]{1,0:T(8,128)}), f32[1024,1024]{1,0:T(8,128)}) %all-gather.19.cloned.1.call-update) | async-done | bytes 4194320 | tf_op jit(solution)/shard_map/all_gather | solution.py:62
  346.5 4.7 fusion.23
  351.1 43.0 %all-gather.21.cloned.1.call-done = f32[1024,1024]{1,0:T(8,128)} async-done(((f32[32,1024]{1,0:T(8,128)}), f32[1024,1024]{1,0:T(8,128)}) %all-gather.21.cloned.1.call-update) | async-done | bytes 4194320 | tf_op jit(solution)/shard_map/all_gather | solution.py:63
  394.1 4.8 fusion.56
  419.9 4.8 fusion.65
  431.4 4.7 fusion.24
  459.3 5.0 fusion.64
  467.1 4.8 convolution_bitcast_fusion.1
  474.4 38.6 %all-gather.23.cloned.1.call-done = f32[1024,1024]{1,0:T(8,128)} async-done(((f32[32,1024]{1,0:T(8,128)}), f32[1024,1024]{1,0:T(8,128)}) %all-gather.23.cloned.1.call-update) | async-done | bytes 4194320 | tf_op jit(solution)/shard_map/all_gather | solution.py:64
  513.0 4.8 convolution_bitcast_fusion
  (122 shorter events, 167.9 us)
Async XLA Ops:
  6.5 52.7 %all-gather.27.cloned.1.call-start = ((), (), s32[]{:S(2)}) async-start(), calls=%async_computation.8 | async-start | bytes 4325376 | tf_op jit(solution)/shard_map/all_gather | solution.py:43
  8.8 147.4 %all-gather.11.cloned.1.call-start = ((), (), s32[]{:S(2)}) async-start(), calls=%async_computation | async-start | bytes 4325376 | tf_op jit(solution)/shard_map/all_gather | solution.py:62
  104.2 4.9 collective-permute-start
  109.9 94.0 %all-gather.13.cloned.1.call-start = ((), (), s32[]{:S(2)}) async-start(), calls=%async_computation.1 | async-start | bytes 4325376 | tf_op jit(solution)/shard_map/all_gather | solution.py:63
  110.6 140.8 %all-gather.15.cloned.1.call-start = ((), (), s32[]{:S(2)}) async-start(), calls=%async_computation.2 | async-start | bytes 4325376 | tf_op jit(solution)/shard_map/all_gather | solution.py:64
  118.0 3.9 collective-permute-start.1
  122.7 176.3 %all-gather.17.cloned.1.call-start = ((), (), s32[]{:S(2)}) async-start(), calls=%async_computation.3 | async-start | bytes 4325376 | tf_op jit(solution)/shard_map/all_gather | solution.py:65
  123.3 223.2 %all-gather.19.cloned.1.call-start = ((), (), s32[]{:S(2)}) async-start(), calls=%async_computation.4 | async-start | bytes 4325376 | tf_op jit(solution)/shard_map/all_gather | solution.py:62
  203.9 7.3 %copy-start.4 = (f32[1024,1024]{1,0:T(8,128)S(1)}, f32[1024,1024]{1,0:T(8,128)}, u32[]{:S(2)}) copy-start(f32[1024,1024]{1,0:T(8,128)} %all-gather.13.cloned.1.call-done) | copy-start | bytes 12582916
  226.6 24.9 %copy-start.16 = (f32[32,1024]{1,0:T(8,128)S(1)}, f32[32,1024]{1,0:T(8,128)}, u32[]{:S(2)}) copy-start(f32[32,1024]{1,0:T(8,128)} %get-tuple-element.12) | copy-start | bytes 393220
  229.1 34.4 %copy-start.13 = (f32[32,1024]{1,0:T(8,128)S(1)}, f32[32,1024]{1,0:T(8,128)}, u32[]{:S(2)}) copy-start(f32[32,1024]{1,0:T(8,128)} %get-tuple-element.9) | copy-start | bytes 393220
  256.3 6.4 %collective-permute-start.2 = (f32[32,1024]{1,0:T(8,128)S(1)}, f32[32,1024]{1,0:T(8,128)S(1)}, u32[]{:S(2)}, u32[]{:S(2)}) collective-permute-start(f32[32,1024]{1,0:T(8,128)S(1)} %convolution_add_fusion.1), channel_id=1, source_target_pairs={{0,64},{64,0},{32,96},{96,32},{1,65},{65,1},{33,97},{97,33},{2,66}... | collective-permute-start | bytes 393224 | tf_op jit(solution)/shard_map/ppermute | solution.py:16
  263.4 130.7 %all-gather.21.cloned.1.call-start = ((), (), s32[]{:S(2)}) async-start(), calls=%async_computation.5 | async-start | bytes 4325376 | tf_op jit(solution)/shard_map/all_gather | solution.py:63
  263.5 7.3 %copy-start.5 = (f32[1024,1024]{1,0:T(8,128)S(1)}, f32[1024,1024]{1,0:T(8,128)}, u32[]{:S(2)}) copy-start(f32[1024,1024]{1,0:T(8,128)} %all-gather.13.cloned.1.call-done) | copy-start | bytes 12582916
  288.7 10.3 %copy-start.15 = (f32[32,1024]{1,0:T(8,128)S(1)}, f32[32,1024]{1,0:T(8,128)}, u32[]{:S(2)}) copy-start(f32[32,1024]{1,0:T(8,128)} %get-tuple-element.11) | copy-start | bytes 393220
  303.8 6.4 %collective-permute-start.4 = (f32[32,1024]{1,0:T(8,128)S(1)}, f32[32,1024]{1,0:T(8,128)S(1)}, u32[]{:S(2)}, u32[]{:S(2)}) collective-permute-start(f32[32,1024]{1,0:T(8,128)S(1)} %convolution_add_fusion), channel_id=1, source_target_pairs={{0,64},{64,0},{32,96},{96,32},{1,65},{65,1},{33,97},{97,33},{2,66}... | collective-permute-start | bytes 393224 | tf_op jit(solution)/shard_map/ppermute | solution.py:16
  310.9 156.2 %all-gather.25.cloned.1.call-start = ((), (), s32[]{:S(2)}) async-start(), calls=%async_computation.7 | async-start | bytes 4325376 | tf_op jit(solution)/shard_map/all_gather | solution.py:65
  315.7 5.4 %collective-permute-start.3 = (f32[32,1024]{1,0:T(8,128)S(1)}, f32[32,1024]{1,0:T(8,128)S(1)}, u32[]{:S(2)}, u32[]{:S(2)}) collective-permute-start(f32[32,1024]{1,0:T(8,128)S(1)} %fusion.45), channel_id=1, source_target_pairs={{0,64},{64,0},{32,96},{96,32},{1,65},{65,1},{33,97},{97,33},{2,66}... | collective-permute-start | bytes 393224 | tf_op jit(solution)/shard_map/ppermute | solution.py:16
  394.1 7.3 %copy-start.8 = (f32[1024,1024]{1,0:T(8,128)S(1)}, f32[1024,1024]{1,0:T(8,128)}, u32[]{:S(2)}) copy-start(f32[1024,1024]{1,0:T(8,128)} %all-gather.21.cloned.1.call-done) | copy-start | bytes 12582916
  419.9 93.2 %all-gather.23.cloned.1.call-start = ((), (), s32[]{:S(2)}) async-start(), calls=%async_computation.6 | async-start | bytes 4325376 | tf_op jit(solution)/shard_map/all_gather | solution.py:64
  419.9 16.1 %copy-start.7 = (f32[1024,1024]{1,0:T(8,128)S(1)}, f32[1024,1024]{1,0:T(8,128)}, u32[]{:S(2)}) copy-start(f32[1024,1024]{1,0:T(8,128)} %all-gather.19.cloned.1.call-done) | copy-start | bytes 12582916
  424.8 13.8 %copy-start.9 = (f32[1024,1024]{1,0:T(8,128)S(1)}, f32[1024,1024]{1,0:T(8,128)}, u32[]{:S(2)}) copy-start(f32[1024,1024]{1,0:T(8,128)} %all-gather.21.cloned.1.call-done) | copy-start | bytes 12582916
  424.8 6.6 %collective-permute-start.5 = (f32[32,1024]{1,0:T(8,128)S(1)}, f32[32,1024]{1,0:T(8,128)S(1)}, u32[]{:S(2)}, u32[]{:S(2)}) collective-permute-start(f32[32,1024]{1,0:T(8,128)S(1)} %fusion.65), channel_id=1, source_target_pairs={{0,64},{64,0},{32,96},{96,32},{1,65},{65,1},{33,97},{97,33},{2,66}... | collective-permute-start | bytes 393224 | tf_op jit(solution)/shard_map/ppermute | solution.py:16
  459.3 5.0 copy-start.10
  (8 other events, 39.0 us)
Sparse Core Ops, SparseCore 0:
  9.6 49.5 all-gather.26
  110.0 46.1 all-gather.10
  158.5 45.3 all-gather.12
  206.0 45.4 all-gather.14
  253.6 45.3 all-gather.16
  301.1 45.3 all-gather.18
  348.7 45.3 all-gather.20
  420.0 45.3 all-gather.24
  467.7 45.3 all-gather.22
where the time goes:
time: 537 us; the launch traced here: 528 us
  waiting for transfers between devices  277 us (52%)
  matrix products  214 us (40%)
  between operations  15.5 us (3%)
  starting transfers between devices  15 us (3%)
    dot_general x65, matrix products, product(): jnp.dot(left_side, right_side, precision=lax.Precision.HIGHEST, preferred...  214 us
    all_gather x2, waiting for transfers between devices, local(): lax.all_gather(front_part[3], 'panel', axis=0, tiled=True)  85.9 us
    all_gather x2, waiting for transfers between devices, local(): lax.all_gather(front_part[2], 'panel', axis=0, tiled=True)  58.4 us
    all_gather x2, waiting for transfers between devices, local(): lax.all_gather(back_part[0], 'panel', axis=0, tiled=True)  58.3 us
    all_gather x1, waiting for transfers between devices, local(): refl_full = lax.all_gather(refl_rows, 'panel', axis=0, tiled=True)  48.9 us
    ppermute x6, waiting for transfers between devices, swapped(): return lax.ppermute(block, axis, route)  19 us
    ppermute x6, starting transfers between devices, swapped(): return lax.ppermute(block, axis, route)  14.7 us
  transfers between devices with their start and end apart: 15, of which 14 were waited for; matrix products, arithmetic and copies ran while one was open for 26% of the time, Pallas kernels for 0%

commit v1 on v0

--- a/solution.py
+++ b/solution.py
@@ -4,6 +4,11 @@
 from jax.sharding import PartitionSpec as P
 
 TERMS = 6
+
+
+def tiled_gather(shard, axis, dim):
+    copies = jnp.concatenate([shard] * lax.axis_size(axis), axis=dim)
+    return lax.all_to_all(copies, axis, dim, dim, tiled=True)
 
 
 def swapped(block, axis, bit):
@@ -59,7 +64,7 @@
         front_part = tuple((jnp.where(is_right, partner_blocks[i], blocks[i]) for i in range(4)))
         back_part = tuple((jnp.where(is_right, blocks[i], partner_blocks[i]) for i in range(4)))
         back_refl_full, front_refl_full, front_trans_full, back_trans_full = (
-            lax.all_gather(back_part[0], "panel", axis=0, tiled=True),
+            tiled_gather(back_part[0], "panel", 0),
             lax.all_gather(front_part[3], "panel", axis=0, tiled=True),
             lax.all_gather(front_part[2], "panel", axis=0, tiled=True),
             lax.all_gather(back_part[1], "panel", axis=0, tiled=True),

time: 537 us -> 521 us (0.970)
  waiting for transfers between devices: 277 us -> 205 us
  matrix products: 214 us -> 239 us
  local copies, waits for them, and re-layouts: 1.65 us -> 24.5 us
  starting transfers between devices: 15 us -> 23.4 us
    all_gather x2, waiting for transfers between devices: 58.4 us -> 0.04 us  [local(): lax.all_gather(front_part[2], 'panel', axis=0, tiled=True)]
    all_gather x2 -> x0, waiting for transfers between devices: 58.3 us -> none  [local(): lax.all_gather(back_part[0], 'panel', axis=0, tiled=True)]
    all_to_all x0 -> x2, waiting for transfers between devices: none -> 53.7 us  [tiled_gather(): return lax.all_to_all(copies, axis, dim, dim, tiled=True)]
    all_gather x2, waiting for transfers between devices: 85.9 us -> 45.1 us  [local(): lax.all_gather(front_part[3], 'panel', axis=0, tiled=True)]
    all_gather x2, waiting for transfers between devices: 5.28 us -> 31.6 us  [local(): lax.all_gather(back_part[1], 'panel', axis=0, tiled=True)]
    dot_general x65, matrix products: 214 us -> 239 us  [product(): jnp.dot(left_side, right_side, precision=lax.Precision.HIGHEST, preferred...]
    unnamed x34 -> x86, local copies, waits for them, and re-layouts: 0.07 us -> 22.2 us
    all_to_all x0 -> x2, starting transfers between devices: none -> 16.1 us  [tiled_gather(): return lax.all_to_all(copies, axis, dim, dim, tiled=True)]
  transfers between devices with their start and end apart: 15 -> 15, of which waited for: 14 -> 9; matrix products, arithmetic and copies ran while one was open for 26% -> 37% of each run, Pallas kernels for 0% -> 0%
where the time goes in v1:
time: 521 us; the launch traced here: 511 us
  matrix products  239 us (46%)
  waiting for transfers between devices  205 us (39%)
  local copies, waits for them, and re-layouts  24.5 us (5%)
  starting transfers between devices  23.4 us (4%)
  between operations  16 us (3%)
    dot_general x65, matrix products, product(): jnp.dot(left_side, right_side, precision=lax.Precision.HIGHEST, preferred...  239 us
    all_to_all x2, waiting for transfers between devices, tiled_gather(): return lax.all_to_all(copies, axis, dim, dim, tiled=True)  53.7 us
    all_gather x1, waiting for transfers between devices, local(): refl_full = lax.all_gather(refl_rows, 'panel', axis=0, tiled=True)  48.9 us
    all_gather x2, waiting for transfers between devices, local(): lax.all_gather(front_part[3], 'panel', axis=0, tiled=True)  45.1 us
    all_gather x2, waiting for transfers between devices, local(): lax.all_gather(back_part[1], 'panel', axis=0, tiled=True)  31.6 us
    ppermute x6, waiting for transfers between devices, swapped(): return lax.ppermute(block, axis, route)  24.5 us
    unnamed x86, local copies, waits for them, and re-layouts  22.2 us
    all_to_all x2, starting transfers between devices, tiled_gather(): return lax.all_to_all(copies, axis, dim, dim, tiled=True)  16.1 us
  transfers between devices with their start and end apart: 15, of which 9 were waited for; matrix products, arithmetic and copies ran while one was open for 37% of the time, Pallas kernels for 0%

profile of v1, /device:TPU:1, one launch (start us, length us, event | category | flops | bytes accessed | tf_op | source)
XLA Modules:
  0.0 511.3 jit_solution(3906614833304534534)
XLA Ops:
  10.3 48.9 %all-gather.21.cloned.1.call-done = f32[1,1024,1024]{2,1,0:T(8,128)} async-done(((f32[1,32,1024]{2,1,0:T(8,128)}), f32[1,1024,1024]{2,1,0:T(8,128)}) %all-gather.21.cloned.1.call-update) | async-done | bytes 4194320 | tf_op jit(solution)/shard_map/all_gather | solution.py:48
  59.2 5.0 fusion.10
  97.4 4.8 fusion.2
  130.0 7.4 %all-to-all-start = ((f32[32,32,1024]{2,1,0:T(8,128)}), f32[32,32,1024]{2,1,0:T(8,128)}, u32[]{:S(2)}, u32[]{:S(2)}) async-start(f32[32,32,1024]{2,1,0:T(8,128)} %bitcast.155), calls=%async_computation | async-start | bytes 8388608 | tf_op jit(solution)/shard_map/all_to_all | solution.py:11
  138.5 53.7 %all-to-all-done = f32[32,32,1024]{2,1,0:T(8,128)} async-done(((f32[32,32,1024]{2,1,0:T(8,128)}), f32[32,32,1024]{2,1,0:T(8,128)}, u32[]{:S(2)}, u32[]{:S(2)}) %all-to-all-start) | async-done | bytes 4194336 | tf_op jit(solution)/shard_map/all_to_all | solution.py:11
  197.0 4.8 fusion.46
  201.8 4.9 fusion.47
  238.6 4.8 convolution_add_fusion
  249.0 5.0 fusion.37
  263.8 4.9 fusion.41
  288.5 5.7 %collective-permute-done.2 = f32[32,1024]{1,0:T(8,128)S(1)} collective-permute-done((f32[32,1024]{1,0:T(8,128)S(1)}, f32[32,1024]{1,0:T(8,128)S(1)}, u32[]{:S(2)}, u32[]{:S(2)}) %collective-permute-start.2) | collective-permute-done | bytes 131104 | tf_op jit(solution)/shard_map/ppermute | solution.py:21
  296.8 8.6 %all-to-all-start.1 = ((f32[32,32,1024]{2,1,0:T(8,128)}), f32[32,32,1024]{2,1,0:T(8,128)}, u32[]{:S(2)}, u32[]{:S(2)}) async-start(f32[32,32,1024]{2,1,0:T(8,128)} %bitcast.156), calls=%async_computation.1 | async-start | bytes 8388608 | tf_op jit(solution)/shard_map/all_to_all | solution.py:11
  310.7 6.4 %collective-permute-done.5 = f32[32,1024]{1,0:T(8,128)S(1)} collective-permute-done((f32[32,1024]{1,0:T(8,128)S(1)}, f32[32,1024]{1,0:T(8,128)S(1)}, u32[]{:S(2)}, u32[]{:S(2)}) %collective-permute-start.5) | collective-permute-done | bytes 131104 | tf_op jit(solution)/shard_map/ppermute | solution.py:21
  317.1 45.1 %all-gather.15.cloned.1.call-done = f32[1024,1024]{1,0:T(8,128)} async-done(((f32[32,1024]{1,0:T(8,128)}), f32[1024,1024]{1,0:T(8,128)}) %all-gather.15.cloned.1.call-update) | async-done | bytes 4194320 | tf_op jit(solution)/shard_map/all_gather | solution.py:68
  366.9 4.8 fusion.66
  381.4 4.8 fusion.70
  395.9 5.2 %add_add_fusion = (f32[32,1024]{1,0:T(8,128)S(1)}, f32[32,1024]{1,0:T(8,128)}) fusion(f32[32,1024]{1,0:T(8,128)S(1)} %fusion.72, f32[32,1024]{1,0:T(8,128)S(1)} %fusion.70, f32[32,1024]{1,0:T(8,128)S(1)} %fusion.68, f32[32,1024]{1,0:T(8,128)S(1)} %fusion.66, f32[32,1024]{1,0:T(8,128)S(1)} %fusion.65, f32[32,1024]{1,0:T(8,128)S(1)} %collective-permute-done.5, ...), kind=kOutput, calls=%fused_computation.93 | convolution fusion | flops 402882560 | bytes 5373953 | tf_op jit(solution)/shard_map/dot_general | solution.py:25
  401.2 4.8 fusion.45
  406.3 6.3 %collective-permute-done.3 = f32[32,1024]{1,0:T(8,128)S(1)} collective-permute-done((f32[32,1024]{1,0:T(8,128)S(1)}, f32[32,1024]{1,0:T(8,128)S(1)}, u32[]{:S(2)}, u32[]{:S(2)}) %collective-permute-start.3) | collective-permute-done | bytes 131104 | tf_op jit(solution)/shard_map/ppermute | solution.py:21
  441.9 4.8 fusion.63
  449.7 4.8 fusion.64
  457.3 4.8 convolution_bitcast_fusion
  464.6 31.6 %all-gather.19.cloned.1.call-done = f32[1024,1024]{1,0:T(8,128)} async-done(((f32[32,1024]{1,0:T(8,128)}), f32[1024,1024]{1,0:T(8,128)}) %all-gather.19.cloned.1.call-update) | async-done | bytes 4194320 | tf_op jit(solution)/shard_map/all_gather | solution.py:70
  496.2 4.8 convolution_bitcast_fusion.1
  (174 shorter events, 208.3 us)
Async XLA Ops:
  6.5 52.7 %all-gather.21.cloned.1.call-start = ((), (), s32[]{:S(2)}) async-start(), calls=%async_computation.8 | async-start | bytes 4325376 | tf_op jit(solution)/shard_map/all_gather | solution.py:48
  8.8 188.1 %all-gather.9.cloned.1.call-start = ((), (), s32[]{:S(2)}) async-start(), calls=%async_computation.2 | async-start | bytes 4325376 | tf_op jit(solution)/shard_map/all_gather | solution.py:68
  59.2 5.0 copy-start
  91.7 4.9 collective-permute-start
  97.4 141.2 %all-gather.13.cloned.1.call-start = ((), (), s32[]{:S(2)}) async-start(), calls=%async_computation.4 | async-start | bytes 4325376 | tf_op jit(solution)/shard_map/all_gather | solution.py:70
  97.4 4.8 copy-start.1
  104.8 3.9 collective-permute-start.1
  130.0 62.2 %copy-start.10 = (f32[32,1024]{1,0:T(8,128)S(1)}, f32[32,1024]{1,0:T(8,128)}, u32[]{:S(2)}) copy-start(f32[32,1024]{1,0:T(8,128)} %get-tuple-element.14) | copy-start | bytes 393220
  130.0 62.2 %all-to-all-start = ((f32[32,32,1024]{2,1,0:T(8,128)}), f32[32,32,1024]{2,1,0:T(8,128)}, u32[]{:S(2)}, u32[]{:S(2)}) async-start(f32[32,32,1024]{2,1,0:T(8,128)} %bitcast.155), calls=%async_computation | async-start | bytes 8388608 | tf_op jit(solution)/shard_map/all_to_all | solution.py:11
  137.4 59.5 %copy-start.11 = (f32[32,1024]{1,0:T(8,128)S(1)}, f32[32,1024]{1,0:T(8,128)}, u32[]{:S(2)}) copy-start(f32[32,1024]{1,0:T(8,128)} %get-tuple-element.13) | copy-start | bytes 393220
  137.4 146.3 %all-gather.11.cloned.1.call-start = ((), (), s32[]{:S(2)}) async-start(), calls=%async_computation.3 | async-start | bytes 4325376 | tf_op jit(solution)/shard_map/all_gather | solution.py:69
  138.0 224.1 %all-gather.15.cloned.1.call-start = ((), (), s32[]{:S(2)}) async-start(), calls=%async_computation.5 | async-start | bytes 4325376 | tf_op jit(solution)/shard_map/all_gather | solution.py:68
  196.9 9.8 %copy-start.2 = (f32[1024,1024]{1,0:T(8,128)S(1)}, f32[1024,1024]{1,0:T(8,128)}, u32[]{:S(2)}) copy-start(f32[1024,1024]{1,0:T(8,128)} %all-gather.9.cloned.1.call-done) | copy-start | bytes 12582916
  238.6 8.0 %copy-start.3 = (f32[1024,1024]{1,0:T(8,128)S(1)}, f32[1024,1024]{1,0:T(8,128)}, u32[]{:S(2)}) copy-start(f32[1024,1024]{1,0:T(8,128)} %all-gather.9.cloned.1.call-done) | copy-start | bytes 12582916
  243.4 34.9 %collective-permute-start.4 = (f32[32,1024]{1,0:T(8,128)S(1)}, f32[32,1024]{1,0:T(8,128)S(1)}, u32[]{:S(2)}, u32[]{:S(2)}) collective-permute-start(f32[32,1024]{1,0:T(8,128)S(1)} %convolution_add_fusion), channel_id=1, source_target_pairs={{0,64},{64,0},{32,96},{96,32},{1,65},{65,1},{33,97},{97,33},{2,66}... | collective-permute-start | bytes 393224 | tf_op jit(solution)/shard_map/ppermute | solution.py:21
  275.8 7.9 %copy-start.12 = (f32[32,1024]{1,0:T(8,128)S(1)}, f32[32,1024]{1,0:T(8,128)}, u32[]{:S(2)}) copy-start(f32[32,1024]{1,0:T(8,128)} %get-tuple-element.15) | copy-start | bytes 393220
  288.4 5.8 %collective-permute-start.2 = (f32[32,1024]{1,0:T(8,128)S(1)}, f32[32,1024]{1,0:T(8,128)S(1)}, u32[]{:S(2)}, u32[]{:S(2)}) collective-permute-start(f32[32,1024]{1,0:T(8,128)S(1)} %convolution_add_fusion.1), channel_id=1, source_target_pairs={{0,64},{64,0},{32,96},{96,32},{1,65},{65,1},{33,97},{97,33},{2,66}... | collective-permute-start | bytes 393224 | tf_op jit(solution)/shard_map/ppermute | solution.py:21
  296.8 70.0 %all-to-all-start.1 = ((f32[32,32,1024]{2,1,0:T(8,128)}), f32[32,32,1024]{2,1,0:T(8,128)}, u32[]{:S(2)}, u32[]{:S(2)}) async-start(f32[32,32,1024]{2,1,0:T(8,128)} %bitcast.156), calls=%async_computation.1 | async-start | bytes 8388608 | tf_op jit(solution)/shard_map/all_to_all | solution.py:11
  305.5 151.8 %all-gather.17.cloned.1.call-start = ((), (), s32[]{:S(2)}) async-start(), calls=%async_computation.6 | async-start | bytes 4325376 | tf_op jit(solution)/shard_map/all_gather | solution.py:69
  310.2 6.9 %collective-permute-start.5 = (f32[32,1024]{1,0:T(8,128)S(1)}, f32[32,1024]{1,0:T(8,128)S(1)}, u32[]{:S(2)}, u32[]{:S(2)}) collective-permute-start(f32[32,1024]{1,0:T(8,128)S(1)} %fusion.65), channel_id=1, source_target_pairs={{0,64},{64,0},{32,96},{96,32},{1,65},{65,1},{33,97},{97,33},{2,66}... | collective-permute-start | bytes 393224 | tf_op jit(solution)/shard_map/ppermute | solution.py:21
  401.2 95.1 %all-gather.19.cloned.1.call-start = ((), (), s32[]{:S(2)}) async-start(), calls=%async_computation.7 | async-start | bytes 4325376 | tf_op jit(solution)/shard_map/all_gather | solution.py:70
  401.2 16.2 %copy-start.5 = (f32[1024,1024]{1,0:T(8,128)S(1)}, f32[1024,1024]{1,0:T(8,128)}, u32[]{:S(2)}) copy-start(f32[1024,1024]{1,0:T(8,128)} %all-gather.15.cloned.1.call-done) | copy-start | bytes 12582916
  406.0 6.7 %collective-permute-start.3 = (f32[32,1024]{1,0:T(8,128)S(1)}, f32[32,1024]{1,0:T(8,128)S(1)}, u32[]{:S(2)}, u32[]{:S(2)}) collective-permute-start(f32[32,1024]{1,0:T(8,128)S(1)} %fusion.45), channel_id=1, source_target_pairs={{0,64},{64,0},{32,96},{96,32},{1,65},{65,1},{33,97},{97,33},{2,66}... | collective-permute-start | bytes 393224 | tf_op jit(solution)/shard_map/ppermute | solution.py:21
  457.3 4.9 copy-start.7
  (4 other events, 16.5 us)
Sparse Core Ops, SparseCore 0:
  9.6 49.5 all-gather.20
  97.5 46.9 all-gather.8
  146.7 71.7 all-gather.12
  220.6 45.6 all-gather.10
  279.2 82.9 all-gather.14
  401.3 45.3 all-gather.16
  449.8 46.3 all-gather.18
